TPU v7x, 32 devices: a whole 2x2x4 slice. The times are simulated.
32 devices in a mesh: section: 4 (over y, x), expert: 8 (over z, core).
Axes of the slice: x: 2, y: 2, z: 4, core: 2. Of those that a mesh axis runs over, the one named last changes fastest.
Arguments:
- saved_inputs: bfloat16 [4, 2, 96, 3072], P('section', None, 'expert'), may hold values from -6 to 6
- expert_ids: int32 [4, 2, 96, 2], P('section'), may hold values from 0 to 3, all different within a row; in each aligned block of 12 rows (0 to 11, 12 to 23, ..., all dimensions but the last counted through in order) at most 9 rows name the same one
- combine: bfloat16 [4, 2, 96, 2], P('section'), may hold values from 0.19921875 to 1
- top_grad: bfloat16 [2, 96, 3072], P(None, 'expert'), may hold values from -6 to 6
- w_gate: bfloat16 [4, 3072, 32768], P('section', None, 'expert'), may hold values from -0.109375 to 0.109375
- w_up: bfloat16 [4, 3072, 32768], P('section', None, 'expert'), may hold values from -0.109375 to 0.109375
- w_down: bfloat16 [4, 32768, 3072], P('section', 'expert'), may hold values from -0.0625 to 0.0625
Outputs:
- input_grads: bfloat16 [4, 2, 96, 3072], P('section', None, 'expert')
- combine_grads: float32 [4, 2, 96, 2], P('section', None, 'expert')
Inputs may be any that keep to these rules, and one draw needn't show every extreme that they name: `expert_ids`: each token names 2 different experts. Among the 12 tokens of one index of expert in one layer and micro-batch, no expert is named more than 9 times, and some expert reaches 9.
All inputs are finite; a program needn't handle non-finite values.
Results may differ from a plain program's by a relative error of at most 0.018.
Values may be sent and summed in bfloat16 or wider, within the bound.
No kernel may reach another device: no remote copies, remote signals or barrier semaphores. Data moves between devices by JAX's collectives and lax.ppermute only.
A program may use at most 192 MiB of HBM per device.

v0:
```python
import jax
import jax.numpy as jnp
from jax import lax
from jax.sharding import PartitionSpec as P

EXPERTS = 4
CAP = 9


def shifted(shard, axis, by):
    length = lax.axis_size(axis)
    pairs = [(i, i + by) for i in range(length) if 0 <= i + by < length]
    return lax.ppermute(shard, axis, pairs)


def silu_parts(values):
    sig = jax.nn.sigmoid(values)
    return (values * sig, sig * (1.0 + values * (1.0 - sig)))


def slot_tables(chosen, experts, capacity):
    onehot = (chosen[:, :, None] == jnp.arange(experts, dtype=jnp.int32)).astype(jnp.int32)
    before = jnp.cumsum(onehot, axis=1) - onehot
    position = jnp.sum(before * onehot, axis=2)
    same_slot = (
        position[:, None, None, :] == jnp.arange(capacity, dtype=jnp.int32)[None, None, :, None]
    ).astype(jnp.int32)
    return (jnp.transpose(onehot, (0, 2, 1))[:, :, None, :] * same_slot).astype(jnp.float32)


def expert_grads(got_inputs, got_grads, weights, gate_part, lift_part, down_part):
    senders, capacity, width = got_inputs.shape
    inputs = got_inputs.reshape(senders * capacity, width)
    grads = got_grads.reshape(senders * capacity, width)
    pre_gate = jnp.dot(inputs, gate_part, preferred_element_type=jnp.float32)
    pre_lift = jnp.dot(inputs, lift_part, preferred_element_type=jnp.float32)
    hidden_grad = jnp.einsum("rd,fd->rf", grads, down_part, preferred_element_type=jnp.float32)
    active, slope = silu_parts(pre_gate)
    slot_grads = jnp.sum(hidden_grad * active * pre_lift, axis=-1)
    scaled = weights.reshape(-1)[:, None] * hidden_grad
    gate_grad = (scaled * pre_lift * slope).astype(jnp.bfloat16)
    lift_grad = (scaled * active).astype(jnp.bfloat16)
    moved = jnp.einsum("rf,df->rd", gate_grad, gate_part, preferred_element_type=jnp.float32)
    moved = moved + jnp.einsum(
        "rf,df->rd", lift_grad, lift_part, preferred_element_type=jnp.float32
    )
    return (moved.reshape(senders, capacity, width), slot_grads.reshape(senders, capacity))


def per_device(saved_inputs, expert_ids, combine, top_grad, w_gate, w_up, w_down):
    devices = lax.axis_size("expert")
    sections = lax.axis_size("section")
    my_index = lax.axis_index("expert")
    my_section = lax.axis_index("section")
    gate_part = w_gate[0]
    lift_part = w_up[0]
    down_part = w_down[0]
    micro = saved_inputs.shape[1]
    tokens = saved_inputs.shape[2]
    width = saved_inputs.shape[3]
    choose = expert_ids.shape[3]
    experts = EXPERTS
    capacity = CAP
    group = devices // experts
    own_expert = my_index // group
    grads_out = jnp.zeros(saved_inputs.shape[1:], jnp.bfloat16)
    slots_out = jnp.zeros((micro, tokens, choose), jnp.float32)
    passed = jnp.zeros((tokens, width), jnp.bfloat16)
    for step in range(micro + sections - 1):
        index = step - (sections - 1 - my_section)
        valid = (index >= 0) & (index < micro)
        current = jnp.clip(index, 0, micro - 1)
        inputs_now = lax.dynamic_index_in_dim(saved_inputs[0], current, 0, keepdims=False)
        from_top = lax.dynamic_index_in_dim(top_grad, current, 0, keepdims=False)
        upper = jnp.where(my_section == sections - 1, from_top, passed)
        chosen = lax.dynamic_index_in_dim(expert_ids[0], current, 0, keepdims=False).reshape(
            devices, tokens * choose
        )
        weights_all = (
            lax.dynamic_index_in_dim(combine[0], current, 0, keepdims=False)
            .reshape(devices, tokens * choose)
            .astype(jnp.float32)
        )
        tables = slot_tables(chosen, experts, capacity)
        recv_table = lax.dynamic_index_in_dim(tables, own_expert, 1, keepdims=False)
        recv_weights = jnp.einsum(
            "jcr,jr->jc", recv_table, weights_all, precision=lax.Precision.HIGHEST
        )
        send_table = lax.dynamic_index_in_dim(tables, my_index, 0, keepdims=False)
        place = jnp.sum(send_table.reshape(experts, capacity, tokens, choose), axis=3)
        place_half = place.astype(jnp.bfloat16)
        sent_inputs = jnp.einsum(
            "ect,td->ecd", place_half, inputs_now, preferred_element_type=jnp.float32
        ).astype(jnp.bfloat16)
        sent_grads = jnp.einsum(
            "ect,td->ecd", place_half, upper, preferred_element_type=jnp.float32
        ).astype(jnp.bfloat16)
        sent_inputs = jnp.repeat(sent_inputs, group, axis=0)
        sent_grads = jnp.repeat(sent_grads, group, axis=0)
        got_inputs, got_grads = (
            lax.all_to_all(sent_inputs, "expert", split_axis=0, concat_axis=0, tiled=True),
            lax.all_to_all(sent_grads, "expert", split_axis=0, concat_axis=0, tiled=True),
        )

        def active_case(first, second):
            return expert_grads(first, second, recv_weights, gate_part, lift_part, down_part)

        def empty_case(first, second):
            return (
                jnp.zeros((devices, capacity, width), jnp.float32),
                jnp.zeros((devices, capacity), jnp.float32),
            )

        part_moved, part_slots = lax.cond(valid, active_case, empty_case, got_inputs, got_grads)
        moved_half = part_moved.astype(jnp.bfloat16)
        slots_half = part_slots.astype(jnp.bfloat16)
        back_moved, back_slots = (
            lax.all_to_all(moved_half, "expert", split_axis=0, concat_axis=0, tiled=True),
            lax.all_to_all(slots_half, "expert", split_axis=0, concat_axis=0, tiled=True),
        )
        back_moved = jnp.sum(
            back_moved.astype(jnp.float32).reshape(experts, group, capacity, width), axis=1
        )
        back_slots = jnp.sum(
            back_slots.astype(jnp.float32).reshape(experts, group, capacity), axis=1
        )
        moved = jnp.einsum("ect,ecd->td", place, back_moved, precision=lax.Precision.HIGHEST)
        slot_grad = jnp.einsum(
            "ecr,ec->r", send_table, back_slots, precision=lax.Precision.HIGHEST
        ).reshape(tokens, choose)
        result = (upper.astype(jnp.float32) + moved).astype(jnp.bfloat16)
        old_grad = lax.dynamic_index_in_dim(grads_out, current, 0, keepdims=False)
        grads_out = lax.dynamic_update_index_in_dim(
            grads_out, jnp.where(valid, result, old_grad), current, 0
        )
        old_slots = lax.dynamic_index_in_dim(slots_out, current, 0, keepdims=False)
        slots_out = lax.dynamic_update_index_in_dim(
            slots_out, jnp.where(valid, slot_grad, old_slots), current, 0
        )
        passed = shifted(result, "section", -1)
    return (grads_out[None], slots_out[None])


def solution(mesh):
    placed = (
        P("section", None, "expert", None),
        P("section", None, None, None),
        P("section", None, None, None),
        P(None, "expert", None),
        P("section", None, "expert"),
        P("section", None, "expert"),
        P("section", "expert", None),
    )
    return jax.shard_map(
        per_device,
        mesh=mesh,
        in_specs=placed,
        out_specs=(P("section", None, "expert", None), P("section", None, "expert", None)),
        check_vma=False,
    )
```

profile of v0, /device:TPU:0, one launch (start us, length us, event | category | flops | bytes accessed | tf_op | source)
XLA Modules:
  0.0 705.3 jit_solution(5870007492429476042)
XLA Ops:
  17.1 16.6 %all-to-all-done = bf16[8,9,3072]{2,1,0:T(8,128)(2,1)S(1)} async-done(((bf16[8,9,3072]{2,1,0:T(8,128)(2,1)}), bf16[8,9,3072]{2,1,0:T(8,128)(2,1)S(1)}, u32[]{:S(2)}, u32[]{:S(2)}) %all-to-all-start) | async-done | bytes 442400 | tf_op jit(solution)/shard_map/all_to_all | solution.py:102
  40.3 18.8 %all-to-all-done.1 = bf16[8,9,3072]{2,1,0:T(8,128)(2,1)S(1)} async-done(((bf16[8,9,3072]{2,1,0:T(8,128)(2,1)}), bf16[8,9,3072]{2,1,0:T(8,128)(2,1)S(1)}, u32[]{:S(2)}, u32[]{:S(2)}) %all-to-all-start.1) | async-done | bytes 442400 | tf_op jit(solution)/shard_map/all_to_all | solution.py:101
  69.2 19.0 %all-to-all-done.2 = bf16[8,9,3072]{2,1,0:T(8,128)(2,1)S(1)} async-done(((bf16[8,9,3072]{2,1,0:T(8,128)(2,1)}), bf16[8,9,3072]{2,1,0:T(8,128)(2,1)S(1)}, u32[]{:S(2)}, u32[]{:S(2)}) %all-to-all-start.2) | async-done | bytes 442400 | tf_op jit(solution)/shard_map/all_to_all | solution.py:118
  101.9 11.7 %all-to-all-done.4 = bf16[8,9,3072]{2,1,0:T(8,128)(2,1)S(1)} async-done(((bf16[8,9,3072]{2,1,0:T(8,128)(2,1)}), bf16[8,9,3072]{2,1,0:T(8,128)(2,1)S(1)}, u32[]{:S(2)}, u32[]{:S(2)}) %all-to-all-start.4) | async-done | bytes 442400 | tf_op jit(solution)/shard_map/all_to_all | solution.py:101
  121.8 17.3 %all-to-all-done.3 = bf16[8,9,3072]{2,1,0:T(8,128)(2,1)S(1)} async-done(((bf16[8,9,3072]{2,1,0:T(8,128)(2,1)}), bf16[8,9,3072]{2,1,0:T(8,128)(2,1)S(1)}, u32[]{:S(2)}, u32[]{:S(2)}) %all-to-all-start.3) | async-done | bytes 442400 | tf_op jit(solution)/shard_map/all_to_all | solution.py:102
  147.6 20.0 %all-to-all-done.5 = bf16[8,9,3072]{2,1,0:T(8,128)(2,1)S(1)} async-done(((bf16[8,9,3072]{2,1,0:T(8,128)(2,1)}), bf16[8,9,3072]{2,1,0:T(8,128)(2,1)S(1)}, u32[]{:S(2)}, u32[]{:S(2)}) %all-to-all-start.5) | async-done | bytes 442400 | tf_op jit(solution)/shard_map/all_to_all | solution.py:118
  181.4 11.7 %all-to-all-done.7 = bf16[8,9,3072]{2,1,0:T(8,128)(2,1)S(1)} async-done(((bf16[8,9,3072]{2,1,0:T(8,128)(2,1)}), bf16[8,9,3072]{2,1,0:T(8,128)(2,1)S(1)}, u32[]{:S(2)}, u32[]{:S(2)}) %all-to-all-start.7) | async-done | bytes 442400 | tf_op jit(solution)/shard_map/all_to_all | solution.py:101
  200.5 17.9 %all-to-all-done.6 = bf16[8,9,3072]{2,1,0:T(8,128)(2,1)S(1)} async-done(((bf16[8,9,3072]{2,1,0:T(8,128)(2,1)}), bf16[8,9,3072]{2,1,0:T(8,128)(2,1)S(1)}, u32[]{:S(2)}, u32[]{:S(2)}) %all-to-all-start.6) | async-done | bytes 442400 | tf_op jit(solution)/shard_map/all_to_all | solution.py:102
  228.6 18.4 %all-to-all-done.8 = bf16[8,9,3072]{2,1,0:T(8,128)(2,1)S(1)} async-done(((bf16[8,9,3072]{2,1,0:T(8,128)(2,1)}), bf16[8,9,3072]{2,1,0:T(8,128)(2,1)S(1)}, u32[]{:S(2)}, u32[]{:S(2)}) %all-to-all-start.8) | async-done | bytes 442400 | tf_op jit(solution)/shard_map/all_to_all | solution.py:118
  255.3 17.0 %all-to-all-done.10 = bf16[8,9,3072]{2,1,0:T(8,128)(2,1)S(1)} async-done(((bf16[8,9,3072]{2,1,0:T(8,128)(2,1)}), bf16[8,9,3072]{2,1,0:T(8,128)(2,1)S(1)}, u32[]{:S(2)}, u32[]{:S(2)}) %all-to-all-start.10) | async-done | bytes 442400 | tf_op jit(solution)/shard_map/all_to_all | solution.py:101
  275.6 141.7 %collective-permute-done.2 = bf16[12,3072]{1,0:T(8,128)(2,1)S(1)} collective-permute-done((bf16[12,3072]{1,0:T(8,128)(2,1)S(1)}, bf16[12,3072]{1,0:T(8,128)(2,1)S(1)}, u32[]{:S(2)}, u32[]{:S(2)}) %collective-permute-start.2) | collective-permute-done | bytes 73760 | tf_op jit(solution)/shard_map/ppermute | solution.py:13
  424.3 19.9 %all-to-all-done.9 = bf16[8,9,3072]{2,1,0:T(8,128)(2,1)S(1)} async-done(((bf16[8,9,3072]{2,1,0:T(8,128)(2,1)}), bf16[8,9,3072]{2,1,0:T(8,128)(2,1)S(1)}, u32[]{:S(2)}, u32[]{:S(2)}) %all-to-all-start.9) | async-done | bytes 442400 | tf_op jit(solution)/shard_map/all_to_all | solution.py:102
  447.4 63.8 %conditional.8 = (bf16[8,9,3072]{2,1,0:T(8,128)(2,1)}, bf16[8,9]{1,0:T(8,128)(2,1)}) conditional(s32[]{:T(128)} %convert_element_type.358, () %tuple.54, (f32[8,9]{1,0:T(8,128)S(1)}, bf16[8,9,3072]{2,1,0:T(8,128)(2,1)S(1)}, bf16[4096,3072]{1,0:T(8,128)(2,1)}, bf16[8,9,3072]{2,1,0:T(8,128)(2,1)S(1)}, bf16[3072,4096]{1,0:T(8,128)(2,1)}, ...), branch_computations={%region_24.25_spmd, %region_25.27_spmd} | conditional | flops 9067511808 | bytes 147359952 | solution.py:114
  459.1 12.5 %fusion.138 = f32[72,4096]{1,0:T(8,128)S(1)} fusion(bf16[72,3072]{1,0:T(8,128)(2,1)S(1)} %reshape.292, bf16[4096,3072]{1,0:T(8,128)(2,1)} %get-tuple-element.80), kind=kOutput, calls=%fused_computation.272 | convolution fusion | flops 1811939328 | bytes 26787840 | tf_op jit(solution)/shard_map/cond/branch_1_fun/rd,fd->rf/dot_general | solution.py:37
  482.9 13.5 %fusion.25 = f32[72,3072]{1,0:T(8,128)} fusion(bf16[3072,4096]{1,0:T(8,128)(2,1)} %get-tuple-element.83, f32[72,4096]{1,0:T(8,128)S(1)} %fusion.139, f32[72,4096]{1,0:T(8,128)S(1)} %get-tuple-element.133, f32[72,4096]{1,0:T(8,128)S(1)} %fusion.138, f32[72]{0:T(128)S(1)} %mul.208), kind=kOutput, calls=%fused_computation.42 | convolution fusion | flops 1815183360 | bytes 29589792 | tf_op jit(solution)/shard_map/cond/branch_1_fun/rf,df->rd/dot_general | solution.py:43
  496.4 12.9 %convolution_add_fusion.3 = bf16[72,3072]{1,0:T(8,128)(2,1)S(1)} fusion(f32[72,3072]{1,0:T(8,128)} %fusion.25, bf16[3072,4096]{1,0:T(8,128)(2,1)} %get-tuple-element.82, f32[72,4096]{1,0:T(8,128)S(1)} %fusion.138, f32[72]{0:T(128)S(1)} %mul.208, f32[72,4096]{1,0:T(8,128)S(1)} %fusion.139), kind=kOutput, calls=%fused_computation.36 | convolution fusion | flops 1814446080 | bytes 28852512 | tf_op jit(solution)/shard_map/cond/branch_1_fun/rf,df->rd/dot_general | solution.py:44
  518.5 18.9 %all-to-all-done.11 = bf16[8,9,3072]{2,1,0:T(8,128)(2,1)S(1)} async-done(((bf16[8,9,3072]{2,1,0:T(8,128)(2,1)}), bf16[8,9,3072]{2,1,0:T(8,128)(2,1)S(1)}, u32[]{:S(2)}, u32[]{:S(2)}) %all-to-all-start.11) | async-done | bytes 442400 | tf_op jit(solution)/shard_map/all_to_all | solution.py:118
  545.2 17.6 %all-to-all-done.13 = bf16[8,9,3072]{2,1,0:T(8,128)(2,1)S(1)} async-done(((bf16[8,9,3072]{2,1,0:T(8,128)(2,1)}), bf16[8,9,3072]{2,1,0:T(8,128)(2,1)S(1)}, u32[]{:S(2)}, u32[]{:S(2)}) %all-to-all-start.13) | async-done | bytes 442400 | tf_op jit(solution)/shard_map/all_to_all | solution.py:101
  586.0 19.8 %all-to-all-done.12 = bf16[8,9,3072]{2,1,0:T(8,128)(2,1)S(1)} async-done(((bf16[8,9,3072]{2,1,0:T(8,128)(2,1)}), bf16[8,9,3072]{2,1,0:T(8,128)(2,1)S(1)}, u32[]{:S(2)}, u32[]{:S(2)}) %all-to-all-start.12) | async-done | bytes 442400 | tf_op jit(solution)/shard_map/all_to_all | solution.py:102
  605.8 63.3 %conditional.9 = (bf16[8,9,3072]{2,1,0:T(8,128)(2,1)}, bf16[8,9]{1,0:T(8,128)(2,1)S(1)}) conditional(s32[]{:T(128)} %convert_element_type.369, () %tuple.56, (f32[8,9]{1,0:T(8,128)S(1)}, bf16[8,9,3072]{2,1,0:T(8,128)(2,1)S(1)}, bf16[4096,3072]{1,0:T(8,128)(2,1)}, bf16[8,9,3072]{2,1,0:T(8,128)(2,1)S(1)}, bf16[3072,4096]{1,0:T(8,128)(2,1)}, ...), branch_computations={%region_31.32_spmd, %region_32.34_spmd} | conditional | flops 9067511808 | bytes 147359952 | solution.py:114
  617.1 12.5 %fusion.140 = f32[72,4096]{1,0:T(8,128)S(1)} fusion(bf16[72,3072]{1,0:T(8,128)(2,1)S(1)} %reshape.296, bf16[4096,3072]{1,0:T(8,128)(2,1)} %get-tuple-element.86), kind=kOutput, calls=%fused_computation.274 | convolution fusion | flops 1811939328 | bytes 26787840 | tf_op jit(solution)/shard_map/cond/branch_1_fun/rd,fd->rf/dot_general | solution.py:37
  641.0 13.5 %fusion.33 = f32[72,3072]{1,0:T(8,128)} fusion(bf16[3072,4096]{1,0:T(8,128)(2,1)} %get-tuple-element.89, f32[72,4096]{1,0:T(8,128)S(1)} %fusion.141, f32[72,4096]{1,0:T(8,128)S(1)} %get-tuple-element.135, f32[72,4096]{1,0:T(8,128)S(1)} %fusion.140, f32[72]{0:T(128)S(1)} %mul.219), kind=kOutput, calls=%fused_computation.54 | convolution fusion | flops 1815183360 | bytes 29589792 | tf_op jit(solution)/shard_map/cond/branch_1_fun/rf,df->rd/dot_general | solution.py:43
  654.6 13.0 %convolution_add_fusion.4 = bf16[72,3072]{1,0:T(8,128)(2,1)S(1)} fusion(f32[72,3072]{1,0:T(8,128)} %fusion.33, bf16[3072,4096]{1,0:T(8,128)(2,1)} %get-tuple-element.88, f32[72,4096]{1,0:T(8,128)S(1)} %fusion.140, f32[72]{0:T(128)S(1)} %mul.219, f32[72,4096]{1,0:T(8,128)S(1)} %fusion.141), kind=kOutput, calls=%fused_computation.48 | convolution fusion | flops 1814446080 | bytes 28852512 | tf_op jit(solution)/shard_map/cond/branch_1_fun/rf,df->rd/dot_general | solution.py:44
  682.7 20.3 %all-to-all-done.14 = bf16[8,9,3072]{2,1,0:T(8,128)(2,1)S(1)} async-done(((bf16[8,9,3072]{2,1,0:T(8,128)(2,1)}), bf16[8,9,3072]{2,1,0:T(8,128)(2,1)S(1)}, u32[]{:S(2)}, u32[]{:S(2)}) %all-to-all-start.14) | async-done | bytes 442400 | tf_op jit(solution)/shard_map/all_to_all | solution.py:118
  (356 shorter events, 219.6 us)
Async XLA Ops:
  6.3 27.4 %all-to-all-start = ((bf16[8,9,3072]{2,1,0:T(8,128)(2,1)}), bf16[8,9,3072]{2,1,0:T(8,128)(2,1)S(1)}, u32[]{:S(2)}, u32[]{:S(2)}) async-start(bf16[8,9,3072]{2,1,0:T(8,128)(2,1)} %bitcast.16), calls=%async_computation | async-start | bytes 1572864 | tf_op jit(solution)/shard_map/all_to_all | solution.py:102
  34.7 24.4 %all-to-all-start.1 = ((bf16[8,9,3072]{2,1,0:T(8,128)(2,1)}), bf16[8,9,3072]{2,1,0:T(8,128)(2,1)S(1)}, u32[]{:S(2)}, u32[]{:S(2)}) async-start(bf16[8,9,3072]{2,1,0:T(8,128)(2,1)} %bitcast.20), calls=%async_computation.1 | async-start | bytes 1572864 | tf_op jit(solution)/shard_map/all_to_all | solution.py:101
  63.6 24.6 %all-to-all-start.2 = ((bf16[8,9,3072]{2,1,0:T(8,128)(2,1)}), bf16[8,9,3072]{2,1,0:T(8,128)(2,1)S(1)}, u32[]{:S(2)}, u32[]{:S(2)}) async-start(bf16[8,9,3072]{2,1,0:T(8,128)(2,1)} %get-tuple-element.102), calls=%async_computation.2 | async-start | bytes 1572864 | tf_op jit(solution)/shard_map/all_to_all | solution.py:118
  89.2 24.4 %all-to-all-start.4 = ((bf16[8,9,3072]{2,1,0:T(8,128)(2,1)}), bf16[8,9,3072]{2,1,0:T(8,128)(2,1)S(1)}, u32[]{:S(2)}, u32[]{:S(2)}) async-start(bf16[8,9,3072]{2,1,0:T(8,128)(2,1)} %bitcast.35), calls=%async_computation.4 | async-start | bytes 1572864 | tf_op jit(solution)/shard_map/all_to_all | solution.py:101
  94.6 7.0 collective-permute-start
  114.6 24.6 %all-to-all-start.3 = ((bf16[8,9,3072]{2,1,0:T(8,128)(2,1)}), bf16[8,9,3072]{2,1,0:T(8,128)(2,1)S(1)}, u32[]{:S(2)}, u32[]{:S(2)}) async-start(bf16[8,9,3072]{2,1,0:T(8,128)(2,1)} %bitcast.32), calls=%async_computation.3 | async-start | bytes 1572864 | tf_op jit(solution)/shard_map/all_to_all | solution.py:102
  143.1 24.6 %all-to-all-start.5 = ((bf16[8,9,3072]{2,1,0:T(8,128)(2,1)}), bf16[8,9,3072]{2,1,0:T(8,128)(2,1)S(1)}, u32[]{:S(2)}, u32[]{:S(2)}) async-start(bf16[8,9,3072]{2,1,0:T(8,128)(2,1)} %get-tuple-element.103), calls=%async_computation.5 | async-start | bytes 1572864 | tf_op jit(solution)/shard_map/all_to_all | solution.py:118
  168.6 24.4 %all-to-all-start.7 = ((bf16[8,9,3072]{2,1,0:T(8,128)(2,1)}), bf16[8,9,3072]{2,1,0:T(8,128)(2,1)S(1)}, u32[]{:S(2)}, u32[]{:S(2)}) async-start(bf16[8,9,3072]{2,1,0:T(8,128)(2,1)} %bitcast.49), calls=%async_computation.7 | async-start | bytes 1572864 | tf_op jit(solution)/shard_map/all_to_all | solution.py:101
  174.1 7.0 collective-permute-start.1
  194.0 24.4 %all-to-all-start.6 = ((bf16[8,9,3072]{2,1,0:T(8,128)(2,1)}), bf16[8,9,3072]{2,1,0:T(8,128)(2,1)S(1)}, u32[]{:S(2)}, u32[]{:S(2)}) async-start(bf16[8,9,3072]{2,1,0:T(8,128)(2,1)} %bitcast.46), calls=%async_computation.6 | async-start | bytes 1572864 | tf_op jit(solution)/shard_map/all_to_all | solution.py:102
  222.4 24.6 %all-to-all-start.8 = ((bf16[8,9,3072]{2,1,0:T(8,128)(2,1)}), bf16[8,9,3072]{2,1,0:T(8,128)(2,1)S(1)}, u32[]{:S(2)}, u32[]{:S(2)}) async-start(bf16[8,9,3072]{2,1,0:T(8,128)(2,1)} %get-tuple-element.104), calls=%async_computation.8 | async-start | bytes 1572864 | tf_op jit(solution)/shard_map/all_to_all | solution.py:118
  247.9 24.4 %all-to-all-start.10 = ((bf16[8,9,3072]{2,1,0:T(8,128)(2,1)}), bf16[8,9,3072]{2,1,0:T(8,128)(2,1)S(1)}, u32[]{:S(2)}, u32[]{:S(2)}) async-start(bf16[8,9,3072]{2,1,0:T(8,128)(2,1)} %bitcast.63), calls=%async_computation.10 | async-start | bytes 1572864 | tf_op jit(solution)/shard_map/all_to_all | solution.py:101
  253.4 163.8 %collective-permute-start.2 = (bf16[12,3072]{1,0:T(8,128)(2,1)S(1)}, bf16[12,3072]{1,0:T(8,128)(2,1)S(1)}, u32[]{:S(2)}, u32[]{:S(2)}) collective-permute-start(bf16[12,3072]{1,0:T(8,128)(2,1)S(1)} %get-tuple-element.123), channel_id=1, source_target_pairs={{8,0},{16,8},{24,16},{9,1},{17,9},{25,17},{10,2},{18,10},{26,18},{... | collective-permute-start | bytes 221192 | tf_op jit(solution)/shard_map/ppermute | solution.py:13
  272.4 145.2 %all-to-all-start.15 = ((bf16[8,1,9]{2,1,0:T(2,128)(2,1)}), bf16[8,1,9]{2,1,0:T(2,128)(2,1)S(1)}, u32[]{:S(2)}, u32[]{:S(2)}) async-start(bf16[8,1,9]{2,1,0:T(2,128)(2,1)} %copy.218), calls=%async_computation.15 | async-start | bytes 8192 | tf_op jit(solution)/shard_map/all_to_all | solution.py:119
  418.5 25.7 %all-to-all-start.9 = ((bf16[8,9,3072]{2,1,0:T(8,128)(2,1)}), bf16[8,9,3072]{2,1,0:T(8,128)(2,1)S(1)}, u32[]{:S(2)}, u32[]{:S(2)}) async-start(bf16[8,9,3072]{2,1,0:T(8,128)(2,1)} %bitcast.60), calls=%async_computation.9 | async-start | bytes 1572864 | tf_op jit(solution)/shard_map/all_to_all | solution.py:102
  444.2 67.1 %all-to-all-start.16 = ((bf16[8,1,9]{2,1,0:T(2,128)(2,1)}), bf16[8,1,9]{2,1,0:T(2,128)(2,1)S(1)}, u32[]{:S(2)}, u32[]{:S(2)}) async-start(bf16[8,1,9]{2,1,0:T(2,128)(2,1)} %copy.220), calls=%async_computation.16 | async-start | bytes 8192 | tf_op jit(solution)/shard_map/all_to_all | solution.py:119
  511.3 26.1 %all-to-all-start.11 = ((bf16[8,9,3072]{2,1,0:T(8,128)(2,1)}), bf16[8,9,3072]{2,1,0:T(8,128)(2,1)S(1)}, u32[]{:S(2)}, u32[]{:S(2)}) async-start(bf16[8,9,3072]{2,1,0:T(8,128)(2,1)} %get-tuple-element.105), calls=%async_computation.11 | async-start | bytes 1572864 | tf_op jit(solution)/shard_map/all_to_all | solution.py:118
  538.4 24.4 %all-to-all-start.13 = ((bf16[8,9,3072]{2,1,0:T(8,128)(2,1)}), bf16[8,9,3072]{2,1,0:T(8,128)(2,1)S(1)}, u32[]{:S(2)}, u32[]{:S(2)}) async-start(bf16[8,9,3072]{2,1,0:T(8,128)(2,1)} %bitcast.78), calls=%async_computation.13 | async-start | bytes 1572864 | tf_op jit(solution)/shard_map/all_to_all | solution.py:101
  543.9 31.0 %collective-permute-start.3 = (bf16[12,3072]{1,0:T(8,128)(2,1)S(1)}, bf16[12,3072]{1,0:T(8,128)(2,1)S(1)}, u32[]{:S(2)}, u32[]{:S(2)}) collective-permute-start(bf16[12,3072]{1,0:T(8,128)(2,1)S(1)} %get-tuple-element.121), channel_id=1, source_target_pairs={{8,0},{16,8},{24,16},{9,1},{17,9},{25,17},{10,2},{18,10},{26,18},{... | collective-permute-start | bytes 221192 | tf_op jit(solution)/shard_map/ppermute | solution.py:13
  562.8 8.7 %all-to-all-start.17 = ((bf16[8,1,9]{2,1,0:T(2,128)(2,1)}), bf16[8,1,9]{2,1,0:T(2,128)(2,1)S(1)}, u32[]{:S(2)}, u32[]{:S(2)}) async-start(bf16[8,1,9]{2,1,0:T(2,128)(2,1)} %copy.222), calls=%async_computation.17 | async-start | bytes 8192 | tf_op jit(solution)/shard_map/all_to_all | solution.py:119
  571.5 8.9 %all-to-all-start.18 = ((bf16[8,1,9]{2,1,0:T(2,128)(2,1)}), bf16[8,1,9]{2,1,0:T(2,128)(2,1)S(1)}, u32[]{:S(2)}, u32[]{:S(2)}) async-start(bf16[8,1,9]{2,1,0:T(2,128)(2,1)} %copy.224), calls=%async_computation.18 | async-start | bytes 8192 | tf_op jit(solution)/shard_map/all_to_all | solution.py:119
  581.4 24.4 %all-to-all-start.12 = ((bf16[8,9,3072]{2,1,0:T(8,128)(2,1)}), bf16[8,9,3072]{2,1,0:T(8,128)(2,1)S(1)}, u32[]{:S(2)}, u32[]{:S(2)}) async-start(bf16[8,9,3072]{2,1,0:T(8,128)(2,1)} %bitcast.75), calls=%async_computation.12 | async-start | bytes 1572864 | tf_op jit(solution)/shard_map/all_to_all | solution.py:102
  669.7 8.9 %all-to-all-start.19 = ((bf16[8,1,9]{2,1,0:T(2,128)(2,1)}), bf16[8,1,9]{2,1,0:T(2,128)(2,1)S(1)}, u32[]{:S(2)}, u32[]{:S(2)}) async-start(bf16[8,1,9]{2,1,0:T(2,128)(2,1)} %copy.226), calls=%async_computation.19 | async-start | bytes 8192 | tf_op jit(solution)/shard_map/all_to_all | solution.py:119
  678.6 24.4 %all-to-all-start.14 = ((bf16[8,9,3072]{2,1,0:T(8,128)(2,1)}), bf16[8,9,3072]{2,1,0:T(8,128)(2,1)S(1)}, u32[]{:S(2)}, u32[]{:S(2)}) async-start(bf16[8,9,3072]{2,1,0:T(8,128)(2,1)} %get-tuple-element.106), calls=%async_computation.14 | async-start | bytes 1572864 | tf_op jit(solution)/shard_map/all_to_all | solution.py:118
  (78 other events, 1082.5 us)
where the time goes:
time: 711 us; the launch traced here: 705 us
  waiting for transfers between devices  431 us (61%)
  matrix products  132 us (19%)
  starting transfers between devices  81 us (11%)
  local copies, waits for them, and re-layouts  37.3 us (5%)
  loops' own time  10.9 us (2%)
  other arithmetic  10.1 us (1%)
    ppermute x4, waiting for transfers between devices, shifted(): return lax.ppermute(shard, axis, pairs)  153 us
    all_to_all x5, waiting for transfers between devices, per_device(): lax.all_to_all(moved_half, 'expert', split_axis=0, concat_axis=0, tiled=T...  96.6 us
    all_to_all x5, waiting for transfers between devices, per_device(): lax.all_to_all(sent_grads, 'expert', split_axis=0, concat_axis=0, tiled=T...  91.5 us
    all_to_all x5, waiting for transfers between devices, per_device(): lax.all_to_all(sent_inputs, 'expert', split_axis=0, concat_axis=0, tiled=...  76.9 us
    dot_general x2, matrix products, expert_grads(): jnp.einsum('rf,df->rd', gate_grad, gate_part, preferred_element_type=jnp....  27.1 us
    dot_general x2, matrix products, expert_grads(): jnp.einsum('rf,df->rd', lift_grad, lift_part, preferred_element_type=jnp....  25.9 us
    dot_general x2, matrix products, expert_grads(): jnp.einsum('rd,fd->rf', grads, down_part, preferred_element_type=jnp.floa...  25.1 us
    dot_general x2, matrix products, expert_grads(): pre_lift = jnp.dot(inputs, lift_part, preferred_element_type=jnp.float32)  22.5 us
  transfers between devices with their start and end apart: 24, of which 21 were waited for; matrix products, arithmetic and copies ran while one was open for 13% of the time, Pallas kernels for 0%

commit v1 on v0

--- a/solution.py
+++ b/solution.py
@@ -5,6 +5,22 @@
 
 EXPERTS = 4
 CAP = 9
+
+
+def swapped_with_each(x, axis, split, join):
+    ways, here = (lax.axis_size(axis), lax.axis_index(axis))
+    width = x.shape[split] // ways
+    dims = list(x.shape)
+    dims[split] = width
+    height = dims[join]
+    dims[join] = height * ways
+    full = jnp.zeros(dims, x.dtype)
+    for mask in range(ways):
+        part = lax.dynamic_slice_in_dim(x, (here ^ mask) * width, width, axis=split)
+        if mask:
+            part = lax.ppermute(part, axis, [(d, d ^ mask) for d in range(ways)])
+        full = lax.dynamic_update_slice_in_dim(full, part, (here ^ mask) * height, axis=join)
+    return full
 
 
 def shifted(shard, axis, by):
@@ -99,7 +115,7 @@
         sent_grads = jnp.repeat(sent_grads, group, axis=0)
         got_inputs, got_grads = (
             lax.all_to_all(sent_inputs, "expert", split_axis=0, concat_axis=0, tiled=True),
-            lax.all_to_all(sent_grads, "expert", split_axis=0, concat_axis=0, tiled=True),
+            swapped_with_each(sent_grads, "expert", 0, 0),
         )
 
         def active_case(first, second):

time: 711 us -> 683 us (0.961)
  waiting for transfers between devices: 431 us -> 355 us
  starting transfers between devices: 81 us -> 116 us
    all_to_all x5 -> x0, waiting for transfers between devices: 91.5 us -> none  [per_device(): lax.all_to_all(sent_grads, 'expert', split_axis=0, concat_axis=0, tiled=T...]
    all_to_all x5, waiting for transfers between devices: 76.9 us -> 4.32 us  [per_device(): lax.all_to_all(sent_inputs, 'expert', split_axis=0, concat_axis=0, tiled=...]
    ppermute x4, waiting for transfers between devices: 153 us -> 201 us  [shifted(): return lax.ppermute(shard, axis, pairs)]
    ppermute x0 -> x35, waiting for transfers between devices: none -> 45.5 us  [swapped_with_each(): part = lax.ppermute(part, axis, [(d, d ^ mask) for d in range(ways)])]
    ppermute x0 -> x35, starting transfers between devices: none -> 43.5 us  [swapped_with_each(): part = lax.ppermute(part, axis, [(d, d ^ mask) for d in range(ways)])]
    all_to_all x5 -> x0, starting transfers between devices: 22 us -> none  [per_device(): lax.all_to_all(sent_grads, 'expert', split_axis=0, concat_axis=0, tiled=T...]
  transfers between devices with their start and end apart: 24 -> 54, of which waited for: 21 -> 24; matrix products, arithmetic and copies ran while one was open for 13% -> 16% of each run, Pallas kernels for 0% -> 0%
where the time goes in v1:
time: 683 us; the launch traced here: 676 us
  waiting for transfers between devices  355 us (52%)
  matrix products  137 us (20%)
  starting transfers between devices  116 us (17%)
  local copies, waits for them, and re-layouts  42.6 us (6%)
  loops' own time  11.7 us (2%)
  other arithmetic  10.8 us (2%)
    ppermute x4, waiting for transfers between devices, shifted(): return lax.ppermute(shard, axis, pairs)  201 us
    all_to_all x5, waiting for transfers between devices, per_device(): lax.all_to_all(moved_half, 'expert', split_axis=0, concat_axis=0, tiled=T...  92.6 us
    ppermute x35, waiting for transfers between devices, swapped_with_each(): part = lax.ppermute(part, axis, [(d, d ^ mask) for d in range(ways)])  45.5 us
    ppermute x35, starting transfers between devices, swapped_with_each(): part = lax.ppermute(part, axis, [(d, d ^ mask) for d in range(ways)])  43.5 us
    dot_general x2, matrix products, expert_grads(): jnp.einsum('rf,df->rd', gate_grad, gate_part, preferred_element_type=jnp....  27.1 us
    all_to_all x5, starting transfers between devices, per_device(): lax.all_to_all(moved_half, 'expert', split_axis=0, concat_axis=0, tiled=T...  26.1 us
    dot_general x2, matrix products, expert_grads(): jnp.einsum('rf,df->rd', lift_grad, lift_part, preferred_element_type=jnp....  26 us
    dot_general x2, matrix products, expert_grads(): jnp.einsum('rd,fd->rf', grads, down_part, preferred_element_type=jnp.floa...  25.1 us
  transfers between devices with their start and end apart: 54, of which 24 were waited for; matrix products, arithmetic and copies ran while one was open for 16% of the time, Pallas kernels for 0%

profile of v1, /device:TPU:0, one launch (start us, length us, event | category | flops | bytes accessed | tf_op | source)
XLA Modules:
  0.0 676.3 jit_solution(14403043887169482954)
XLA Ops:
  31.7 8.2 %collective-permute-done.5 = bf16[1,9,3072]{2,1,0:T(8,128)(2,1)S(1)} collective-permute-done((bf16[1,9,3072]{2,1,0:T(8,128)(2,1)S(1)}, bf16[1,9,3072]{2,1,0:T(8,128)(2,1)S(1)}, u32[]{:S(2)}, u32[]{:S(2)}) %collective-permute-start.5) | collective-permute-done | bytes 55328 | tf_op jit(solution)/shard_map/ppermute | solution.py:21
  59.2 17.5 %all-to-all-done.1 = bf16[8,9,3072]{2,1,0:T(8,128)(2,1)S(1)} async-done(((bf16[8,9,3072]{2,1,0:T(8,128)(2,1)}), bf16[8,9,3072]{2,1,0:T(8,128)(2,1)S(1)}, u32[]{:S(2)}, u32[]{:S(2)}) %all-to-all-start.1) | async-done | bytes 442400 | tf_op jit(solution)/shard_map/all_to_all | solution.py:134
  99.4 13.7 %collective-permute-done.11 = bf16[1,9,3072]{2,1,0:T(8,128)(2,1)S(1)} collective-permute-done((bf16[1,9,3072]{2,1,0:T(8,128)(2,1)S(1)}, bf16[1,9,3072]{2,1,0:T(8,128)(2,1)S(1)}, u32[]{:S(2)}, u32[]{:S(2)}) %collective-permute-start.11) | collective-permute-done | bytes 55328 | tf_op jit(solution)/shard_map/ppermute | solution.py:21
  128.2 19.1 %all-to-all-done.3 = bf16[8,9,3072]{2,1,0:T(8,128)(2,1)S(1)} async-done(((bf16[8,9,3072]{2,1,0:T(8,128)(2,1)}), bf16[8,9,3072]{2,1,0:T(8,128)(2,1)S(1)}, u32[]{:S(2)}, u32[]{:S(2)}) %all-to-all-start.3) | async-done | bytes 442400 | tf_op jit(solution)/shard_map/all_to_all | solution.py:134
  199.8 17.0 %all-to-all-done.5 = bf16[8,9,3072]{2,1,0:T(8,128)(2,1)S(1)} async-done(((bf16[8,9,3072]{2,1,0:T(8,128)(2,1)}), bf16[8,9,3072]{2,1,0:T(8,128)(2,1)S(1)}, u32[]{:S(2)}, u32[]{:S(2)}) %all-to-all-start.5) | async-done | bytes 442400 | tf_op jit(solution)/shard_map/all_to_all | solution.py:134
  230.1 179.4 %collective-permute-done.23 = bf16[12,3072]{1,0:T(8,128)(2,1)S(1)} collective-permute-done((bf16[12,3072]{1,0:T(8,128)(2,1)S(1)}, bf16[12,3072]{1,0:T(8,128)(2,1)S(1)}, u32[]{:S(2)}, u32[]{:S(2)}) %collective-permute-start.23) | collective-permute-done | bytes 73760 | tf_op jit(solution)/shard_map/ppermute | solution.py:29
  429.0 67.3 %conditional.8 = (bf16[8,9,3072]{2,1,0:T(8,128)(2,1)}, bf16[8,9]{1,0:T(8,128)(2,1)}) conditional(s32[]{:T(128)} %convert_element_type.378, () %tuple.74, (f32[8,9]{1,0:T(8,128)}, bf16[8,9,3072]{2,1,0:T(8,128)(2,1)S(1)}, s32[]{:T(128)}, bf16[1,9,3072]{2,1,0:T(8,128)(2,1)S(1)}, s32[]{:T(128)}, /*index=5*/bf16[1,9,3072]{2,1,0:T(8,128)(2,1)S(1)}, ...), branch_computations={%region_24.25_spmd, %region_25.27_spmd} | conditional | flops 9067511808 | bytes 151144912 | solution.py:130
  430.1 10.6 %fusion.139 = f32[72,4096]{1,0:T(8,128)S(1)} fusion(bf16[72,3072]{1,0:T(8,128)(2,1)S(1)} %reshape.333, bf16[3072,4096]{1,0:T(8,128)(2,1)} %get-tuple-element.893), kind=kOutput, calls=%fused_computation.348 | convolution fusion | flops 1811939328 | bytes 26787840 | tf_op jit(solution)/shard_map/cond/branch_1_fun/dot_general | solution.py:51
  442.8 12.5 %fusion.138 = f32[72,4096]{1,0:T(8,128)S(1)} fusion(bf16[72,3072]{1,0:T(8,128)(2,1)} %reshape.332, bf16[4096,3072]{1,0:T(8,128)(2,1)} %get-tuple-element.890), kind=kOutput, calls=%fused_computation.347 | convolution fusion | flops 1811939328 | bytes 26787840 | tf_op jit(solution)/shard_map/cond/branch_1_fun/rd,fd->rf/dot_general | solution.py:53
  455.3 11.2 %multiply_reduce_fusion.3 = (bf16[72]{0:T(256)(128)(2,1)}, f32[72,4096]{1,0:T(8,128)S(1)}) fusion(f32[72,4096]{1,0:T(8,128)S(1)} %fusion.138, f32[72,4096]{1,0:T(8,128)S(1)} %fusion.139, bf16[72,3072]{1,0:T(8,128)(2,1)S(1)} %copy-done.7, bf16[3072,4096]{1,0:T(8,128)(2,1)} %get-tuple-element.892), kind=kOutput, calls=%fused_computation.61 | convolution fusion | flops 1814003584 | bytes 29147280 | tf_op jit(solution)/shard_map/cond/branch_1_fun/dot_general | solution.py:52
  467.9 13.5 %fusion.25 = f32[72,3072]{1,0:T(8,128)} fusion(bf16[3072,4096]{1,0:T(8,128)(2,1)} %get-tuple-element.893, f32[72,4096]{1,0:T(8,128)S(1)} %fusion.139, f32[72,4096]{1,0:T(8,128)S(1)} %get-tuple-element.958, f32[72,4096]{1,0:T(8,128)S(1)} %fusion.138, f32[72]{0:T(128)} %mul.318), kind=kOutput, calls=%fused_computation.66 | convolution fusion | flops 1815183360 | bytes 29589792 | tf_op jit(solution)/shard_map/cond/branch_1_fun/rf,df->rd/dot_general | solution.py:59
  481.4 12.9 %convolution_add_fusion.3 = bf16[72,3072]{1,0:T(8,128)(2,1)S(1)} fusion(f32[72,3072]{1,0:T(8,128)} %fusion.25, bf16[3072,4096]{1,0:T(8,128)(2,1)} %get-tuple-element.892, f32[72,4096]{1,0:T(8,128)S(1)} %fusion.138, f32[72]{0:T(128)} %mul.318, f32[72,4096]{1,0:T(8,128)S(1)} %fusion.139), kind=kOutput, calls=%fused_computation.60 | convolution fusion | flops 1814446080 | bytes 28852512 | tf_op jit(solution)/shard_map/cond/branch_1_fun/rf,df->rd/dot_general | solution.py:60
  496.4 7.3 %all-to-all-start.7 = ((bf16[8,9,3072]{2,1,0:T(8,128)(2,1)}), bf16[8,9,3072]{2,1,0:T(8,128)(2,1)S(1)}, u32[]{:S(2)}, u32[]{:S(2)}) async-start(bf16[8,9,3072]{2,1,0:T(8,128)(2,1)} %get-tuple-element.930), calls=%async_computation.7 | async-start | bytes 1572864 | tf_op jit(solution)/shard_map/all_to_all | solution.py:134
  505.9 18.7 %all-to-all-done.7 = bf16[8,9,3072]{2,1,0:T(8,128)(2,1)S(1)} async-done(((bf16[8,9,3072]{2,1,0:T(8,128)(2,1)}), bf16[8,9,3072]{2,1,0:T(8,128)(2,1)S(1)}, u32[]{:S(2)}, u32[]{:S(2)}) %all-to-all-start.7) | async-done | bytes 442400 | tf_op jit(solution)/shard_map/all_to_all | solution.py:134
  538.0 12.7 %collective-permute-done.31 = bf16[12,3072]{1,0:T(8,128)(2,1)S(1)} collective-permute-done((bf16[12,3072]{1,0:T(8,128)(2,1)S(1)}, bf16[12,3072]{1,0:T(8,128)(2,1)S(1)}, u32[]{:S(2)}, u32[]{:S(2)}) %collective-permute-start.31) | collective-permute-done | bytes 73760 | tf_op jit(solution)/shard_map/ppermute | solution.py:29
  563.9 6.1 collective-permute-done.35
  571.0 65.9 %conditional.9 = (bf16[8,9,3072]{2,1,0:T(8,128)(2,1)}, bf16[8,9]{1,0:T(8,128)(2,1)S(1)}) conditional(s32[]{:T(128)} %convert_element_type.389, () %tuple.76, (f32[8,9]{1,0:T(8,128)S(1)}, bf16[8,9,3072]{2,1,0:T(8,128)(2,1)S(1)}, s32[]{:T(128)}, bf16[1,9,3072]{2,1,0:T(8,128)(2,1)S(1)}, s32[]{:T(128)}, /*index=5*/bf16[1,9,3072]{2,1,0:T(8,128)(2,1)S(1)}, ...), branch_computations={%region_31.32_spmd, %region_32.34_spmd} | conditional | flops 9067511808 | bytes 151144912 | solution.py:130
  572.1 10.6 %fusion.141 = f32[72,4096]{1,0:T(8,128)S(1)} fusion(bf16[72,3072]{1,0:T(8,128)(2,1)S(1)} %reshape.337, bf16[3072,4096]{1,0:T(8,128)(2,1)} %get-tuple-element.914), kind=kOutput, calls=%fused_computation.350 | convolution fusion | flops 1811939328 | bytes 26787840 | tf_op jit(solution)/shard_map/cond/branch_1_fun/dot_general | solution.py:51
  584.9 12.5 %fusion.140 = f32[72,4096]{1,0:T(8,128)S(1)} fusion(bf16[72,3072]{1,0:T(8,128)(2,1)} %reshape.336, bf16[4096,3072]{1,0:T(8,128)(2,1)} %get-tuple-element.911), kind=kOutput, calls=%fused_computation.349 | convolution fusion | flops 1811939328 | bytes 26787840 | tf_op jit(solution)/shard_map/cond/branch_1_fun/rd,fd->rf/dot_general | solution.py:53
  597.4 11.2 %multiply_reduce_fusion.4 = (bf16[72]{0:T(256)(128)(2,1)}, f32[72,4096]{1,0:T(8,128)S(1)}) fusion(f32[72,4096]{1,0:T(8,128)S(1)} %fusion.140, f32[72,4096]{1,0:T(8,128)S(1)} %fusion.141, bf16[72,3072]{1,0:T(8,128)(2,1)S(1)} %copy-done.9, bf16[3072,4096]{1,0:T(8,128)(2,1)} %get-tuple-element.913), kind=kOutput, calls=%fused_computation.81 | convolution fusion | flops 1814003584 | bytes 29147280 | tf_op jit(solution)/shard_map/cond/branch_1_fun/dot_general | solution.py:52
  608.7 13.5 %fusion.33 = f32[72,3072]{1,0:T(8,128)} fusion(bf16[3072,4096]{1,0:T(8,128)(2,1)} %get-tuple-element.914, f32[72,4096]{1,0:T(8,128)S(1)} %fusion.141, f32[72,4096]{1,0:T(8,128)S(1)} %get-tuple-element.960, f32[72,4096]{1,0:T(8,128)S(1)} %fusion.140, f32[72]{0:T(128)S(1)} %mul.329), kind=kOutput, calls=%fused_computation.86 | convolution fusion | flops 1815183360 | bytes 29589792 | tf_op jit(solution)/shard_map/cond/branch_1_fun/rf,df->rd/dot_general | solution.py:59
  622.2 13.1 %convolution_add_fusion.4 = bf16[72,3072]{1,0:T(8,128)(2,1)S(1)} fusion(f32[72,3072]{1,0:T(8,128)} %fusion.33, bf16[3072,4096]{1,0:T(8,128)(2,1)} %get-tuple-element.913, f32[72,4096]{1,0:T(8,128)S(1)} %fusion.140, f32[72]{0:T(128)S(1)} %mul.329, f32[72,4096]{1,0:T(8,128)S(1)} %fusion.141), kind=kOutput, calls=%fused_computation.80 | convolution fusion | flops 1814446080 | bytes 28852512 | tf_op jit(solution)/shard_map/cond/branch_1_fun/rf,df->rd/dot_general | solution.py:60
  637.4 6.3 all-to-all-start.14
  653.4 20.3 %all-to-all-done.9 = bf16[8,9,3072]{2,1,0:T(8,128)(2,1)S(1)} async-done(((bf16[8,9,3072]{2,1,0:T(8,128)(2,1)}), bf16[8,9,3072]{2,1,0:T(8,128)(2,1)S(1)}, u32[]{:S(2)}, u32[]{:S(2)}) %all-to-all-start.9) | async-done | bytes 442400 | tf_op jit(solution)/shard_map/all_to_all | solution.py:134
  (471 shorter events, 228.3 us)
Async XLA Ops:
  5.8 21.2 %collective-permute-start = (bf16[1,9,3072]{2,1,0:T(8,128)(2,1)S(1)}, bf16[1,9,3072]{2,1,0:T(8,128)(2,1)S(1)}, u32[]{:S(2)}, u32[]{:S(2)}) collective-permute-start(bf16[1,9,3072]{2,1,0:T(8,128)(2,1)S(1)} %get-tuple-element.995), channel_id=1, source_target_pairs={{0,1},{1,0},{2,3},{3,2},{4,5},{5,4},{6,7},{7,6},{8,9},{9,8},{10,11... | collective-permute-start | bytes 165896 | tf_op jit(solution)/shard_map/ppermute | solution.py:21
  6.3 24.6 %collective-permute-start.1 = (bf16[1,9,3072]{2,1,0:T(8,128)(2,1)S(1)}, bf16[1,9,3072]{2,1,0:T(8,128)(2,1)S(1)}, u32[]{:S(2)}, u32[]{:S(2)}) collective-permute-start(bf16[1,9,3072]{2,1,0:T(8,128)(2,1)S(1)} %get-tuple-element.994), channel_id=1, source_target_pairs={{0,2},{1,3},{2,0},{3,1},{4,6},{5,7},{6,4},{7,5},{8,10},{9,11},{10,... | collective-permute-start | bytes 165896 | tf_op jit(solution)/shard_map/ppermute | solution.py:21
  8.8 22.8 %collective-permute-start.2 = (bf16[1,9,3072]{2,1,0:T(8,128)(2,1)S(1)}, bf16[1,9,3072]{2,1,0:T(8,128)(2,1)S(1)}, u32[]{:S(2)}, u32[]{:S(2)}) collective-permute-start(bf16[1,9,3072]{2,1,0:T(8,128)(2,1)S(1)} %get-tuple-element.993), channel_id=1, source_target_pairs={{0,3},{1,2},{2,1},{3,0},{4,7},{5,6},{6,5},{7,4},{8,11},{9,10},{10,... | collective-permute-start | bytes 165896 | tf_op jit(solution)/shard_map/ppermute | solution.py:21
  8.9 22.7 %collective-permute-start.3 = (bf16[1,9,3072]{2,1,0:T(8,128)(2,1)S(1)}, bf16[1,9,3072]{2,1,0:T(8,128)(2,1)S(1)}, u32[]{:S(2)}, u32[]{:S(2)}) collective-permute-start(bf16[1,9,3072]{2,1,0:T(8,128)(2,1)S(1)} %get-tuple-element.992), channel_id=1, source_target_pairs={{0,4},{1,5},{2,6},{3,7},{4,0},{5,1},{6,2},{7,3},{8,12},{9,13},{10,... | collective-permute-start | bytes 165896 | tf_op jit(solution)/shard_map/ppermute | solution.py:21
  11.7 20.0 %collective-permute-start.4 = (bf16[1,9,3072]{2,1,0:T(8,128)(2,1)S(1)}, bf16[1,9,3072]{2,1,0:T(8,128)(2,1)S(1)}, u32[]{:S(2)}, u32[]{:S(2)}) collective-permute-start(bf16[1,9,3072]{2,1,0:T(8,128)(2,1)S(1)} %get-tuple-element.991), channel_id=1, source_target_pairs={{0,5},{1,4},{2,7},{3,6},{4,1},{5,0},{6,3},{7,2},{8,13},{9,12},{10,... | collective-permute-start | bytes 165896 | tf_op jit(solution)/shard_map/ppermute | solution.py:21
  14.4 30.7 %all-to-all-start = ((bf16[8,9,3072]{2,1,0:T(8,128)(2,1)}), bf16[8,9,3072]{2,1,0:T(8,128)(2,1)S(1)}, u32[]{:S(2)}, u32[]{:S(2)}) async-start(bf16[8,9,3072]{2,1,0:T(8,128)(2,1)} %bitcast.20), calls=%async_computation | async-start | bytes 1572864 | tf_op jit(solution)/shard_map/all_to_all | solution.py:117
  50.1 26.5 %all-to-all-start.1 = ((bf16[8,9,3072]{2,1,0:T(8,128)(2,1)}), bf16[8,9,3072]{2,1,0:T(8,128)(2,1)S(1)}, u32[]{:S(2)}, u32[]{:S(2)}) async-start(bf16[8,9,3072]{2,1,0:T(8,128)(2,1)} %get-tuple-element.927), calls=%async_computation.1 | async-start | bytes 1572864 | tf_op jit(solution)/shard_map/all_to_all | solution.py:134
  77.6 37.2 %all-to-all-start.2 = ((bf16[8,9,3072]{2,1,0:T(8,128)(2,1)}), bf16[8,9,3072]{2,1,0:T(8,128)(2,1)S(1)}, u32[]{:S(2)}, u32[]{:S(2)}) async-start(bf16[8,9,3072]{2,1,0:T(8,128)(2,1)} %bitcast.35), calls=%async_computation.2 | async-start | bytes 1572864 | tf_op jit(solution)/shard_map/all_to_all | solution.py:117
  91.7 21.5 %collective-permute-start.11 = (bf16[1,9,3072]{2,1,0:T(8,128)(2,1)S(1)}, bf16[1,9,3072]{2,1,0:T(8,128)(2,1)S(1)}, u32[]{:S(2)}, u32[]{:S(2)}) collective-permute-start(bf16[1,9,3072]{2,1,0:T(8,128)(2,1)S(1)} %get-tuple-element.985), channel_id=1, source_target_pairs={{0,4},{1,5},{2,6},{3,7},{4,0},{5,1},{6,2},{7,3},{8,12},{9,13},{10,... | collective-permute-start | bytes 165896 | tf_op jit(solution)/shard_map/ppermute | solution.py:21
  94.3 20.5 %collective-permute-start.12 = (bf16[1,9,3072]{2,1,0:T(8,128)(2,1)S(1)}, bf16[1,9,3072]{2,1,0:T(8,128)(2,1)S(1)}, u32[]{:S(2)}, u32[]{:S(2)}) collective-permute-start(bf16[1,9,3072]{2,1,0:T(8,128)(2,1)S(1)} %get-tuple-element.984), channel_id=1, source_target_pairs={{0,5},{1,4},{2,7},{3,6},{4,1},{5,0},{6,3},{7,2},{8,13},{9,12},{10,... | collective-permute-start | bytes 165896 | tf_op jit(solution)/shard_map/ppermute | solution.py:21
  95.5 19.3 %collective-permute-start.13 = (bf16[1,9,3072]{2,1,0:T(8,128)(2,1)S(1)}, bf16[1,9,3072]{2,1,0:T(8,128)(2,1)S(1)}, u32[]{:S(2)}, u32[]{:S(2)}) collective-permute-start(bf16[1,9,3072]{2,1,0:T(8,128)(2,1)S(1)} %get-tuple-element.983), channel_id=1, source_target_pairs={{0,6},{1,7},{2,4},{3,5},{4,2},{5,3},{6,0},{7,1},{8,14},{9,15},{10,... | collective-permute-start | bytes 165896 | tf_op jit(solution)/shard_map/ppermute | solution.py:21
  122.8 24.6 %all-to-all-start.3 = ((bf16[8,9,3072]{2,1,0:T(8,128)(2,1)}), bf16[8,9,3072]{2,1,0:T(8,128)(2,1)S(1)}, u32[]{:S(2)}, u32[]{:S(2)}) async-start(bf16[8,9,3072]{2,1,0:T(8,128)(2,1)} %get-tuple-element.928), calls=%async_computation.3 | async-start | bytes 1572864 | tf_op jit(solution)/shard_map/all_to_all | solution.py:134
  148.3 26.2 %all-to-all-start.4 = ((bf16[8,9,3072]{2,1,0:T(8,128)(2,1)}), bf16[8,9,3072]{2,1,0:T(8,128)(2,1)S(1)}, u32[]{:S(2)}, u32[]{:S(2)}) async-start(bf16[8,9,3072]{2,1,0:T(8,128)(2,1)} %bitcast.49), calls=%async_computation.4 | async-start | bytes 1572864 | tf_op jit(solution)/shard_map/all_to_all | solution.py:117
  165.3 18.7 %collective-permute-start.19 = (bf16[1,9,3072]{2,1,0:T(8,128)(2,1)S(1)}, bf16[1,9,3072]{2,1,0:T(8,128)(2,1)S(1)}, u32[]{:S(2)}, u32[]{:S(2)}) collective-permute-start(bf16[1,9,3072]{2,1,0:T(8,128)(2,1)S(1)} %get-tuple-element.978), channel_id=1, source_target_pairs={{0,4},{1,5},{2,6},{3,7},{4,0},{5,1},{6,2},{7,3},{8,12},{9,13},{10,... | collective-permute-start | bytes 165896 | tf_op jit(solution)/shard_map/ppermute | solution.py:21
  167.8 17.1 %collective-permute-start.20 = (bf16[1,9,3072]{2,1,0:T(8,128)(2,1)S(1)}, bf16[1,9,3072]{2,1,0:T(8,128)(2,1)S(1)}, u32[]{:S(2)}, u32[]{:S(2)}) collective-permute-start(bf16[1,9,3072]{2,1,0:T(8,128)(2,1)S(1)} %get-tuple-element.977), channel_id=1, source_target_pairs={{0,5},{1,4},{2,7},{3,6},{4,1},{5,0},{6,3},{7,2},{8,13},{9,12},{10,... | collective-permute-start | bytes 165896 | tf_op jit(solution)/shard_map/ppermute | solution.py:21
  167.8 17.1 %collective-permute-start.21 = (bf16[1,9,3072]{2,1,0:T(8,128)(2,1)S(1)}, bf16[1,9,3072]{2,1,0:T(8,128)(2,1)S(1)}, u32[]{:S(2)}, u32[]{:S(2)}) collective-permute-start(bf16[1,9,3072]{2,1,0:T(8,128)(2,1)S(1)} %get-tuple-element.976), channel_id=1, source_target_pairs={{0,6},{1,7},{2,4},{3,5},{4,2},{5,3},{6,0},{7,1},{8,14},{9,15},{10,... | collective-permute-start | bytes 165896 | tf_op jit(solution)/shard_map/ppermute | solution.py:21
  189.7 27.0 %all-to-all-start.5 = ((bf16[8,9,3072]{2,1,0:T(8,128)(2,1)}), bf16[8,9,3072]{2,1,0:T(8,128)(2,1)S(1)}, u32[]{:S(2)}, u32[]{:S(2)}) async-start(bf16[8,9,3072]{2,1,0:T(8,128)(2,1)} %get-tuple-element.929), calls=%async_computation.5 | async-start | bytes 1572864 | tf_op jit(solution)/shard_map/all_to_all | solution.py:134
  221.2 188.2 %collective-permute-start.23 = (bf16[12,3072]{1,0:T(8,128)(2,1)S(1)}, bf16[12,3072]{1,0:T(8,128)(2,1)S(1)}, u32[]{:S(2)}, u32[]{:S(2)}) collective-permute-start(bf16[12,3072]{1,0:T(8,128)(2,1)S(1)} %get-tuple-element.948), channel_id=1, source_target_pairs={{8,0},{16,8},{24,16},{9,1},{17,9},{25,17},{10,2},{18,10},{26,18},{... | collective-permute-start | bytes 221192 | tf_op jit(solution)/shard_map/ppermute | solution.py:29
  226.6 193.0 %all-to-all-start.6 = ((bf16[8,9,3072]{2,1,0:T(8,128)(2,1)}), bf16[8,9,3072]{2,1,0:T(8,128)(2,1)S(1)}, u32[]{:S(2)}, u32[]{:S(2)}) async-start(bf16[8,9,3072]{2,1,0:T(8,128)(2,1)} %bitcast.63), calls=%async_computation.6 | async-start | bytes 1572864 | tf_op jit(solution)/shard_map/all_to_all | solution.py:117
  419.6 76.8 %all-to-all-start.12 = ((bf16[8,1,9]{2,1,0:T(2,128)(2,1)}), bf16[8,1,9]{2,1,0:T(2,128)(2,1)}, u32[]{:S(2)}, u32[]{:S(2)}) async-start(bf16[8,1,9]{2,1,0:T(2,128)(2,1)} %copy.222), calls=%async_computation.12 | async-start | bytes 8192 | tf_op jit(solution)/shard_map/all_to_all | solution.py:135
  496.4 28.2 %all-to-all-start.7 = ((bf16[8,9,3072]{2,1,0:T(8,128)(2,1)}), bf16[8,9,3072]{2,1,0:T(8,128)(2,1)S(1)}, u32[]{:S(2)}, u32[]{:S(2)}) async-start(bf16[8,9,3072]{2,1,0:T(8,128)(2,1)} %get-tuple-element.930), calls=%async_computation.7 | async-start | bytes 1572864 | tf_op jit(solution)/shard_map/all_to_all | solution.py:134
  529.1 21.6 %collective-permute-start.31 = (bf16[12,3072]{1,0:T(8,128)(2,1)S(1)}, bf16[12,3072]{1,0:T(8,128)(2,1)S(1)}, u32[]{:S(2)}, u32[]{:S(2)}) collective-permute-start(bf16[12,3072]{1,0:T(8,128)(2,1)S(1)} %get-tuple-element.946), channel_id=1, source_target_pairs={{8,0},{16,8},{24,16},{9,1},{17,9},{25,17},{10,2},{18,10},{26,18},{... | collective-permute-start | bytes 221192 | tf_op jit(solution)/shard_map/ppermute | solution.py:29
  534.4 29.5 %all-to-all-start.8 = ((bf16[8,9,3072]{2,1,0:T(8,128)(2,1)}), bf16[8,9,3072]{2,1,0:T(8,128)(2,1)S(1)}, u32[]{:S(2)}, u32[]{:S(2)}) async-start(bf16[8,9,3072]{2,1,0:T(8,128)(2,1)} %bitcast.78), calls=%async_computation.8 | async-start | bytes 1572864 | tf_op jit(solution)/shard_map/all_to_all | solution.py:117
  649.3 24.4 %all-to-all-start.9 = ((bf16[8,9,3072]{2,1,0:T(8,128)(2,1)}), bf16[8,9,3072]{2,1,0:T(8,128)(2,1)S(1)}, u32[]{:S(2)}, u32[]{:S(2)}) async-start(bf16[8,9,3072]{2,1,0:T(8,128)(2,1)} %get-tuple-element.931), calls=%async_computation.9 | async-start | bytes 1572864 | tf_op jit(solution)/shard_map/all_to_all | solution.py:134
  (124 other events, 1730.5 us)
